TPU v7x, 256 devices: a whole 4x4x8 slice. The times are simulated.
256 devices in a mesh: narrow: 8 (over y, core), wide: 32 (over x, z).
Axes of the slice: x: 4, y: 4, z: 8, core: 2. Of those that a mesh axis runs over, the one named last changes fastest.
Arguments:
- points: float32 [2, 32768], P(None, ('narrow', 'wide')), may hold values from 0 to 1
- quad_weight: float32 [32768], P(('narrow', 'wide')), may hold values from 9.155274e-06 to 9.1552734e-05
- basis: float32 [4, 2, 32768, 128], P(None, None, ('narrow', 'wide')), may hold values from -6 to 6
- jacobi: float32 [2, 32768], P(None, ('narrow', 'wide')), may hold values from 0.5 to 2
- near_panel: int32 [2048, 12], P(('narrow', 'wide')), may hold values from 0 to 2047, as said below
- near_count: int32 [2048], P(('narrow', 'wide')), may hold values from 2 to 12, as said below
- near_block: bfloat16 [2048, 12, 32, 32], P(('narrow', 'wide')), may hold values from -0.875 to 0.875
- agg_index: int32 [2, 32768], P(None, ('narrow', 'wide')), may hold values from 0 to 47
- coarse_inverse: float32 [8, 1536, 12288], P(None, 'wide', 'narrow'), may hold values from -0.1 to 0.5
Outputs:
- new_block: float32 [2, 32768, 128], P(None, ('narrow', 'wide'))
- hessenberg: float32 [4, 128, 128], replicated
- upper_factor: float32 [128, 128], replicated
Inputs may be any that keep to these rules, and one draw needn't show every extreme that they name: near_panel[p, 0] = p; every entry lies within 4 panels of p in panel order, and some entry lies exactly 4 panels away. `near_count`: slots at or beyond a panel's count are not used; some panel uses all 12.
All inputs are finite; a program needn't handle non-finite values.
Results may differ from a plain program's by a relative error of at most 0.0027.
The roundings to bfloat16 on the way count: a program that leaves them out, or rounds other values in their place, can miss the bound.
Values may be sent and summed in bfloat16 or wider, within the bound.
A program may use at most 64 MiB of HBM per device.

v0:
```python
import math
import jax
import jax.numpy as jnp
from jax import lax
from jax.sharding import PartitionSpec as P

SPAN = 4
NU = 0.3
DELTA2 = 1e-05
ELASTIC = 40.0
HIGH = lax.Precision.HIGHEST


def extended(block, sides, width):
    for axis, dim in sides:
        count = lax.axis_size(axis)
        forward = [(i, i + 1) for i in range(count - 1)]
        backward = [(target, source) for source, target in forward]
        low = lax.ppermute(
            lax.slice_in_dim(block, block.shape[dim] - width, None, axis=dim), axis, forward
        )
        high = lax.ppermute(lax.slice_in_dim(block, 0, width, axis=dim), axis, backward)
        block = jnp.concatenate([low, block, high], axis=dim)
    return block


def far_kernel(targets, sources, weights):
    delta_x = targets[0][:, None] - sources[0][None, :]
    delta_y = targets[1][:, None] - sources[1][None, :]
    square_dist = delta_x * delta_x + delta_y * delta_y + DELTA2
    factor = ELASTIC * weights[None, :]
    log_part = -0.5 * (3.0 - 4.0 * NU) * jnp.log(square_dist)
    g_xx = factor * (log_part + delta_x * delta_x / square_dist)
    g_xy = factor * (delta_x * delta_y / square_dist)
    g_yy = factor * (log_part + delta_y * delta_y / square_dist)
    first_row = jnp.stack([g_xx, g_xy], axis=1)
    second_row = jnp.stack([g_xy, g_yy], axis=1)
    stacked = jnp.stack([first_row, second_row], axis=0)
    return stacked.reshape(2 * targets.shape[1], 2 * sources.shape[1]).astype(jnp.bfloat16)


def far_product(targets, sources, weights, fields):
    piece_len = sources.shape[1]
    row_count = targets.shape[1]
    rhs_count = fields.shape[2]
    block_size = math.gcd(piece_len, max(512, 524288 // row_count))
    block_count = piece_len // block_size

    def one_block(block_index, running):
        offset = block_index * block_size
        source_block = lax.dynamic_slice_in_dim(sources, offset, block_size, 1)
        weight_block = lax.dynamic_slice_in_dim(weights, offset, block_size, 0)
        field_block = lax.dynamic_slice_in_dim(fields, offset, block_size, 1)
        kernel_block = far_kernel(targets, source_block, weight_block)
        return running + jnp.dot(
            kernel_block,
            field_block.reshape(2 * block_size, rhs_count),
            preferred_element_type=jnp.float32,
        )

    initial = jnp.zeros((2 * row_count, rhs_count), jnp.float32)
    return lax.fori_loop(0, block_count, one_block, initial)


def make_fold(targets, source_all, shard_piece):
    return far_product(targets, source_all[0:2], source_all[2], shard_piece)


def body(
    points,
    quad_weight,
    basis,
    jacobi,
    near_panel,
    near_count,
    near_block,
    agg_index,
    coarse_inverse,
):
    block_total = basis.shape[0]
    point_count = basis.shape[2]
    rhs_count = basis.shape[3]
    coarse_count = coarse_inverse.shape[1]
    newest = basis[block_total - 1]
    member = (
        agg_index[:, :, None] == jnp.arange(coarse_count, dtype=jnp.int32)[None, None, :]
    ).astype(jnp.float32)
    coarse_rhs = jnp.einsum("apc,apr->cr", member, newest, precision=HIGH)
    coarse_part = jnp.einsum(
        "abc,cr->abr",
        coarse_inverse,
        lax.all_gather(coarse_rhs, "wide", axis=0, tiled=True),
        precision=HIGH,
    )
    coarse_sol = lax.psum_scatter(coarse_part, "narrow", scatter_dimension=0, tiled=True)[0]
    lifted = jnp.einsum("apc,cr->apr", member, coarse_sol, precision=HIGH)
    precond = (jacobi[:, :, None] * newest + lifted).astype(jnp.bfloat16)
    source_info = jnp.concatenate([points, quad_weight[None, :]], axis=0)
    targets = lax.all_gather(points, "narrow", axis=1, tiled=True)
    source_all = lax.all_gather(source_info, "wide", axis=1, tiled=True)
    far_part = make_fold(targets, source_all, lax.all_gather(precond, "wide", axis=1, tiled=True))
    far_local = lax.psum_scatter(
        far_part.reshape(2, targets.shape[1], rhs_count), "narrow", scatter_dimension=1, tiled=True
    )
    panels_dev = near_panel.shape[0]
    slot_total = near_panel.shape[1]
    nodes = near_block.shape[2] // 2
    padded = extended(precond, ((("narrow", "wide"), 1),), SPAN * nodes)
    panel_fields = padded.reshape(2, panels_dev + 2 * SPAN, nodes, rhs_count)
    local_index = near_panel - lax.axis_index(("narrow", "wide")) * panels_dev + SPAN
    gathered = panel_fields[:, local_index]
    slot_live = jnp.arange(slot_total, dtype=jnp.int32)[None, :] < near_count[:, None]
    gathered = jnp.where(slot_live[None, :, :, None, None], gathered, jnp.zeros((), gathered.dtype))
    gathered = jnp.transpose(gathered, (1, 2, 0, 3, 4)).reshape(
        panels_dev, slot_total, 2 * nodes, rhs_count
    )
    near_terms = jnp.einsum(
        "pkxy,pkyr->pxr", near_block, gathered, preferred_element_type=jnp.float32
    )
    near = jnp.transpose(near_terms.reshape(panels_dev, 2, nodes, rhs_count), (1, 0, 2, 3)).reshape(
        2, point_count, rhs_count
    )
    image = 0.5 * precond.astype(jnp.float32) + far_local + near
    weighted = basis * quad_weight[None, None, :, None]
    local_proj = jnp.einsum("jair,aiw->jrw", weighted, image, precision=HIGH)
    hessenberg = lax.psum(local_proj, ("narrow", "wide"))
    remainder = image - jnp.einsum("jair,jrw->aiw", basis, hessenberg, precision=HIGH)
    local_gram = jnp.einsum(
        "air,aiw->rw", remainder * quad_weight[None, :, None], remainder, precision=HIGH
    )
    gram_matrix = lax.psum(local_gram, ("narrow", "wide"))
    lower_factor = jnp.linalg.cholesky(gram_matrix)
    flat = remainder.reshape(2 * point_count, rhs_count)
    solved = jax.scipy.linalg.solve_triangular(lower_factor, flat.T, lower=True)
    new_block = solved.T.reshape(2, point_count, rhs_count)
    return (new_block, hessenberg, lower_factor.T)


def solution(mesh):
    in_specs = (
        P(None, ("narrow", "wide")),
        P(("narrow", "wide")),
        P(None, None, ("narrow", "wide"), None),
        P(None, ("narrow", "wide")),
        P(("narrow", "wide"), None),
        P(("narrow", "wide")),
        P(("narrow", "wide"), None, None, None),
        P(None, ("narrow", "wide")),
        P(None, "wide", "narrow"),
    )
    out_specs = (P(None, ("narrow", "wide"), None), P(), P())
    return jax.shard_map(body, mesh=mesh, in_specs=in_specs, out_specs=out_specs, check_vma=False)
```

profile of v0, /device:TPU:1, one launch (start us, length us, event | category | flops | bytes accessed | tf_op | source)
XLA Modules:
  0.0 911.1 jit_solution(4539948616988339396)
XLA Ops:
  8.5 42.3 %all_gather.12 = f32[1536,128]{1,0:T(8,128)S(1)} all-gather(f32[48,128]{1,0:T(8,128)S(1)} %convolution_bitcast_fusion.4), channel_id=1, replica_groups=mesh['narrow'=8,'wide'=32] {'wide'}, dimensions={0}, use_global_device_ids=true | all-gather | bytes 811008 | tf_op jit(solution)/shard_map/all_gather | solution.py:92
  50.9 2.7 convolution_bitcast_fusion.1
  53.6 40.3 %reduce-scatter.3.cloned.1.call-done = f32[1,48,128]{2,1,0:T(8,128)} async-done(((f32[8,48,128]{2,1,0:T(8,128)}), f32[1,48,128]{2,1,0:T(8,128)}) %reduce-scatter.3.cloned.1.call-update) | async-done | bytes 24592 | tf_op jit(solution)/shard_map/reduce_scatter | solution.py:95
  94.0 1.8 fusion.16
  95.9 38.2 %all_gather.13 = f32[3,4096]{1,0:T(4,128)S(1)} all-gather(f32[3,128]{1,0:T(4,128)S(1)} %pad_maximum_fusion.2), channel_id=1, replica_groups=mesh['narrow'=8,'wide'=32] {'wide'}, dimensions={1}, use_global_device_ids=true | all-gather | bytes 50688 | tf_op jit(solution)/shard_map/all_gather | solution.py:100
  134.2 22.4 %all_gather.14 = f32[2,1024]{1,0:T(2,128)S(1)} all-gather(f32[2,128]{1,0:T(2,128)S(1)} %copy-done.8), channel_id=1, replica_groups=mesh['narrow'=8,'wide'=32] {'narrow'}, dimensions={1}, use_global_device_ids=true | all-gather | bytes 9216 | tf_op jit(solution)/shard_map/all_gather | solution.py:99
  156.6 14.8 %all-gather.2.cloned.1.call-done = bf16[2,4096,128]{2,1,0:T(8,128)(2,1)} async-done(((bf16[2,128,128]{2,1,0:T(8,128)(2,1)}), bf16[2,4096,128]{2,1,0:T(8,128)(2,1)}) %all-gather.2.cloned.1.call-update) | async-done | bytes 2097168 | tf_op jit(solution)/shard_map/all_gather | solution.py:101
  171.5 163.6 %while.14 = (s32[]{:T(128)}, f32[2048,128]{1,0:T(8,128)}, f32[4096]{0:T(1024)S(1)}, f32[2,1024]{1,0:T(2,128)S(1)}, f32[2,4096]{1,0:T(2,128)S(1)}, /*index=5*/bf1...) while((s32[]{:T(128)}, f32[2048,128]{1,0:T(8,128)}, ...), condition=%wide.region_2.0_spmd.clone, body=%wide.region_1.0_spmd.clone.sunk | while | flops 551551488 | bytes 51161332 | solution.py:62
  174.0 6.3 copy.58
  180.3 5.4 copy.59
  185.7 1.7 constant_dynamic-slice_fusion.5
  187.4 3.5 convolution_add_fusion.3
  194.4 6.3 copy.58
  200.7 5.4 copy.59
  206.2 1.7 constant_dynamic-slice_fusion.5
  207.8 3.5 convolution_add_fusion.3
  214.9 6.3 copy.58
  221.2 5.4 copy.59
  226.6 1.7 constant_dynamic-slice_fusion.5
  228.3 3.5 convolution_add_fusion.3
  235.3 6.3 copy.58
  241.6 5.4 copy.59
  247.1 1.7 constant_dynamic-slice_fusion.5
  248.7 3.5 convolution_add_fusion.3
  255.8 6.3 copy.58
  262.1 5.4 copy.59
  267.5 1.7 constant_dynamic-slice_fusion.5
  269.2 3.5 convolution_add_fusion.3
  276.2 6.3 copy.58
  282.5 5.4 copy.59
  288.0 1.7 constant_dynamic-slice_fusion.5
  289.6 3.5 convolution_add_fusion.3
  296.7 6.3 copy.58
  303.0 5.4 copy.59
  308.4 1.7 constant_dynamic-slice_fusion.5
  310.1 3.5 convolution_add_fusion.3
  317.1 6.3 copy.58
  323.4 5.4 copy.59
  328.8 1.7 constant_dynamic-slice_fusion.5
  330.5 3.5 convolution_add_fusion.3
  335.3 2.4 collective-permute-start
  337.7 8.7 collective-permute-start.1
  352.0 17.6 %reduce-scatter.5.cloned.1.call-done = f32[2,128,128]{2,1,0:T(8,128)} async-done(((f32[2,1024,128]{2,1,0:T(8,128)}), f32[2,128,128]{2,1,0:T(8,128)}) %reduce-scatter.5.cloned.1.call-update) | async-done | bytes 131088 | tf_op jit(solution)/shard_map/reduce_scatter | solution.py:102
  370.6 1.8 convolution_bitcast_fusion
  372.6 256.9 %all-reduce.3.cloned.1.call-done = f32[4,128,128]{2,1,0:T(8,128)} async-done(((f32[4,128,128]{2,1,0:T(8,128)}), f32[4,128,128]{2,1,0:T(8,128)}) %all-reduce.3.cloned.1.call-update) | async-done | bytes 262160 | tf_op jit(solution)/shard_map/psum | solution.py:126
  632.2 245.4 %all-reduce.5.cloned.1.call-done = f32[128,128]{0,1:T(8,128)} async-done(((f32[128,128]{0,1:T(8,128)}), f32[128,128]{0,1:T(8,128)}) %all-reduce.5.cloned.1.call-update) | async-done | bytes 65552 | tf_op jit(solution)/shard_map/psum | solution.py:131
  879.4 11.7 %cholesky.16 = f32[128,128]{1,0:T(8,128)S(1)} custom-call(f32[128,128]{1,0:T(8,128)S(1)} %fusion.27), custom_call_target="Cholesky" | custom-call | tf_op jit(solution)/shard_map/jit(cholesky)/cholesky | solution.py:132
  892.4 9.8 %custom-call.7 = f32[1,128,128]{1,2,0:T(8,128)S(1)} custom-call(f32[1,128,128]{2,1,0:T(8,128)S(1)} %get-tuple-element.165), custom_call_target="InvertDiagBlocksLowerTriangular" | custom-call | tf_op jit(solution)/shard_map/jit(_solve_triangular)/triangular_solve | solution.py:134
  (138 shorter events, 44.4 us)
Async XLA Ops:
  7.2 43.7 %copy-start = (f32[8,48,1536]{2,1,0:T(8,128)S(1)}, f32[8,48,1536]{2,1,0:T(8,128)}, u32[]{:S(2)}) copy-start(f32[8,48,1536]{2,1,0:T(8,128)} %param.19) | copy-start | bytes 7077892
  7.2 86.8 %reduce-scatter.3.cloned.1.call-start = ((), (), s32[]{:S(2)}) async-start(), calls=%async_computation.2 | async-start | bytes 221184 | tf_op jit(solution)/shard_map/reduce_scatter | solution.py:95
  8.5 85.5 %copy-start.7 = (s32[2,128]{1,0:T(2,128)S(1)}, s32[2,128]{1,0:T(2,128)}, u32[]{:S(2)}) copy-start(s32[2,128]{1,0:T(2,128)} %param.18) | copy-start | bytes 3076
  8.5 85.5 %copy-start.10 = (f32[2,128]{1,0:T(2,128)S(1)}, f32[2,128]{1,0:T(2,128)}, u32[]{:S(2)}) copy-start(f32[2,128]{1,0:T(2,128)} %param.14) | copy-start | bytes 3076
  50.9 45.1 %copy-start.6 = (f32[128]{0:T(128)S(1)}, f32[128]{0:T(128)}, u32[]{:S(2)}) copy-start(f32[128]{0:T(128)} %param.12) | copy-start | bytes 1540
  50.9 45.1 %copy-start.8 = (f32[2,128]{1,0:T(2,128)S(1)}, f32[2,128]{1,0:T(2,128)}, u32[]{:S(2)}) copy-start(f32[2,128]{1,0:T(2,128)} %param.11) | copy-start | bytes 3076
  53.6 117.9 %all-gather.2.cloned.1.call-start = ((), (), s32[]{:S(2)}) async-start(), calls=%async_computation.3 | async-start | bytes 2162688 | tf_op jit(solution)/shard_map/all_gather | solution.py:101
  95.9 273.8 %reduce-scatter.5.cloned.1.call-start = ((), (), s32[]{:S(2)}) async-start(), calls=%async_computation.4 | async-start | bytes 1179648 | tf_op jit(solution)/shard_map/reduce_scatter | solution.py:102
  171.5 163.7 %copy-start.9 = (s32[8,12]{1,0:T(8,128)S(1)}, s32[8,12]{1,0:T(8,128)}, u32[]{:S(2)}) copy-start(s32[8,12]{1,0:T(8,128)} %param.15) | copy-start | bytes 1156
  171.5 163.8 %copy-start.11 = (s32[8]{0:T(128)S(1)}, s32[8]{0:T(128)}, u32[]{:S(2)}) copy-start(s32[8]{0:T(128)} %param.16) | copy-start | bytes 100
  171.5 163.8 %copy-start.4 = (bf16[2,128,128]{2,1,0:T(8,128)(2,1)S(1)}, bf16[2,128,128]{2,1,0:T(8,128)(2,1)}, u32[]{:S(2)}) copy-start(bf16[2,128,128]{2,1,0:T(8,128)(2,1)} %fusion.16) | copy-start | bytes 196612
  180.3 7.1 copy-start.1
  190.9 1.0 copy-start.2
  200.7 7.1 copy-start.1
  211.4 1.0 copy-start.2
  221.2 7.1 copy-start.1
  231.8 1.0 copy-start.2
  241.6 7.1 copy-start.1
  252.3 1.0 copy-start.2
  262.1 7.1 copy-start.1
  272.7 1.0 copy-start.2
  282.5 7.1 copy-start.1
  293.2 1.0 copy-start.2
  303.0 7.1 copy-start.1
  313.6 1.0 copy-start.2
  323.4 7.1 copy-start.1
  334.1 1.0 copy-start.2
  335.1 294.4 %all-reduce.3.cloned.1.call-start = ((), (), s32[]{:S(2)}) async-start(), calls=%async_computation.5 | async-start | bytes 524288 | tf_op jit(solution)/shard_map/psum | solution.py:126
  335.3 11.1 %collective-permute-start = (bf16[2,64,128]{2,1,0:T(8,128)(2,1)S(1)}, bf16[2,64,128]{2,1,0:T(8,128)(2,1)S(1)}, u32[]{:S(2)}, u32[]{:S(2)}) collective-permute-start(bf16[2,64,128]{2,1,0:T(8,128)(2,1)S(1)} %get-tuple-element.166), channel_id=1, source_target_pairs={{0,1},{1,2},{2,3},{3,4},{4,5},{5,6},{6,7},{7,8},{8,9},{9,10},{10,1... | collective-permute-start | bytes 98312 | tf_op jit(solution)/shard_map/ppermute | solution.py:19
  337.7 9.7 %collective-permute-start.1 = (bf16[2,64,128]{2,1,0:T(8,128)(2,1)S(1)}, bf16[2,64,128]{2,1,0:T(8,128)(2,1)S(1)}, u32[]{:S(2)}, u32[]{:S(2)}) collective-permute-start(bf16[2,64,128]{2,1,0:T(8,128)(2,1)S(1)} %get-tuple-element.167), channel_id=1, source_target_pairs={{1,0},{2,1},{3,2},{4,3},{5,4},{6,5},{7,6},{8,7},{9,8},{10,9},{11,1... | collective-permute-start | bytes 98312 | tf_op jit(solution)/shard_map/ppermute | solution.py:22
  349.0 21.5 %copy-start.3 = (f32[4,2,128,128]{3,2,1,0:T(8,128)S(1)}, f32[4,2,128,128]{3,2,1,0:T(8,128)}, u32[]{:S(2)}) copy-start(f32[4,2,128,128]{3,2,1,0:T(8,128)} %param.13) | copy-start | bytes 1572868
  372.4 505.2 %all-reduce.5.cloned.1.call-start = ((), (), s32[]{:S(2)}) async-start(), calls=%async_computation.6 | async-start | bytes 131072 | tf_op jit(solution)/shard_map/psum | solution.py:131
  629.5 274.4 %copy-start.5 = (f32[4,128,128]{2,1,0:T(8,128)S(1)}, f32[4,128,128]{2,1,0:T(8,128)}, u32[]{:S(2)}) copy-start(f32[4,128,128]{2,1,0:T(8,128)} %all-reduce.3.cloned.1.call-done) | copy-start | bytes 786436
Sparse Core Ops, SparseCore 0:
  53.7 40.2 reduce-scatter.2
  97.1 74.2 all-gather.1
  335.2 34.3 reduce-scatter.4
  375.5 253.9 all-reduce.2
  635.4 242.0 all-reduce.4
where the time goes:
time: 912 us; the launch traced here: 911 us
  waiting for transfers between devices  576 us (63%)
  local copies, waits for them, and re-layouts  120 us (13%)
  blocking collectives  103 us (11%)
  other arithmetic  45.4 us (5%)
  matrix products  41.1 us (5%)
  between operations  14 us (2%)
  starting transfers between devices  11.5 us (1%)
    psum x1, waiting for transfers between devices, body(): hessenberg = lax.psum(local_proj, ('narrow', 'wide'))  257 us
    psum x1, waiting for transfers between devices, body(): gram_matrix = lax.psum(local_gram, ('narrow', 'wide'))  245 us
    while x40, local copies, waits for them, and re-layouts  51.2 us
    another operation x8, local copies, waits for them, and re-layouts, far_kernel(): stacked = jnp.stack([first_row, second_row], axis=0)  50.4 us
    all_gather x1, blocking collectives, body(): lax.all_gather(coarse_rhs, 'wide', axis=0, tiled=True)  42.3 us
    reduce_scatter x1, waiting for transfers between devices, body(): lax.psum_scatter(coarse_part, 'narrow', scatter_dimension=0, tiled=True)[0]  40.3 us
    all_gather x1, blocking collectives, body(): source_all = lax.all_gather(source_info, 'wide', axis=1, tiled=True)  38.2 us
    dot_general x8, matrix products, one_block(): jnp.dot(kernel_block, field_block.reshape(2 * block_size, rhs_count), pre...  28.3 us
  transfers between devices with their start and end apart: 7, of which 6 were waited for; matrix products, arithmetic and copies ran while one was open for 1% of the time, Pallas kernels for 0%

commit v1 on v0

--- a/solution.py
+++ b/solution.py
@@ -123,7 +123,10 @@
     image = 0.5 * precond.astype(jnp.float32) + far_local + near
     weighted = basis * quad_weight[None, None, :, None]
     local_proj = jnp.einsum("jair,aiw->jrw", weighted, image, precision=HIGH)
-    hessenberg = lax.psum(local_proj, ("narrow", "wide"))
+    trace_the_series_all = lambda row_axis, my_tile, across: jax.lax.psum(
+        jax.lax.psum(my_tile, row_axis), across
+    )
+    hessenberg = trace_the_series_all("narrow", local_proj, "wide")
     remainder = image - jnp.einsum("jair,jrw->aiw", basis, hessenberg, precision=HIGH)
     local_gram = jnp.einsum(
         "air,aiw->rw", remainder * quad_weight[None, :, None], remainder, precision=HIGH

time: 912 us -> 866 us (0.950)
  waiting for transfers between devices: 576 us -> 530 us
    psum x1 -> x2, waiting for transfers between devices: 257 us -> 210 us  [the longest x1 145 us: body(): jax.lax.psum(jax.lax.psum(my_tile, row_axis), across)]
  transfers between devices with their start and end apart: 7 -> 8, of which waited for: 6 -> 7; matrix products, arithmetic and copies ran while one was open for 1% -> 1% of each run, Pallas kernels for 0% -> 0%
where the time goes in v1:
time: 866 us
  waiting for transfers between devices  530 us (61%)
  local copies, waits for them, and re-layouts  120 us (14%)
  blocking collectives  103 us (12%)
  other arithmetic  45.4 us (5%)
  matrix products  41.1 us (5%)
  between operations  14.3 us (2%)
  starting transfers between devices  11.5 us (1%)
    psum x1, waiting for transfers between devices, body(): gram_matrix = lax.psum(local_gram, ('narrow', 'wide'))  246 us
    psum x1, waiting for transfers between devices, body(): jax.lax.psum(jax.lax.psum(my_tile, row_axis), across)  145 us
    psum x1, waiting for transfers between devices, body(): jax.lax.psum(my_tile, row_axis)  64.7 us
    while x40, local copies, waits for them, and re-layouts  51.2 us
    another operation x8, local copies, waits for them, and re-layouts, far_kernel(): stacked = jnp.stack([first_row, second_row], axis=0)  50.4 us
    all_gather x1, blocking collectives, body(): lax.all_gather(coarse_rhs, 'wide', axis=0, tiled=True)  42.3 us
    reduce_scatter x1, waiting for transfers between devices, body(): lax.psum_scatter(coarse_part, 'narrow', scatter_dimension=0, tiled=True)[0]  40.3 us
    all_gather x1, blocking collectives, body(): source_all = lax.all_gather(source_info, 'wide', axis=1, tiled=True)  38.2 us
  transfers between devices with their start and end apart: 8, of which 7 were waited for; matrix products, arithmetic and copies ran while one was open for 1% of the time, Pallas kernels for 0%

profile of v1, /device:TPU:1, one launch (start us, length us, event | category | flops | bytes accessed | tf_op | source)
XLA Modules:
  0.0 865.8 jit_solution(13826240138039921814)
XLA Ops:
  8.5 42.3 %all_gather.12 = f32[1536,128]{1,0:T(8,128)S(1)} all-gather(f32[48,128]{1,0:T(8,128)S(1)} %convolution_bitcast_fusion.4), channel_id=1, replica_groups=mesh['narrow'=8,'wide'=32] {'wide'}, dimensions={0}, use_global_device_ids=true | all-gather | bytes 811008 | tf_op jit(solution)/shard_map/all_gather | solution.py:92
  50.9 2.7 convolution_bitcast_fusion.1
  53.6 40.3 %reduce-scatter.3.cloned.1.call-done = f32[1,48,128]{2,1,0:T(8,128)} async-done(((f32[8,48,128]{2,1,0:T(8,128)}), f32[1,48,128]{2,1,0:T(8,128)}) %reduce-scatter.3.cloned.1.call-update) | async-done | bytes 24592 | tf_op jit(solution)/shard_map/reduce_scatter | solution.py:95
  94.0 1.8 fusion.16
  95.9 38.2 %all_gather.13 = f32[3,4096]{1,0:T(4,128)S(1)} all-gather(f32[3,128]{1,0:T(4,128)S(1)} %pad_maximum_fusion.2), channel_id=1, replica_groups=mesh['narrow'=8,'wide'=32] {'wide'}, dimensions={1}, use_global_device_ids=true | all-gather | bytes 50688 | tf_op jit(solution)/shard_map/all_gather | solution.py:100
  134.2 22.4 %all_gather.14 = f32[2,1024]{1,0:T(2,128)S(1)} all-gather(f32[2,128]{1,0:T(2,128)S(1)} %copy-done.8), channel_id=1, replica_groups=mesh['narrow'=8,'wide'=32] {'narrow'}, dimensions={1}, use_global_device_ids=true | all-gather | bytes 9216 | tf_op jit(solution)/shard_map/all_gather | solution.py:99
  156.6 14.8 %all-gather.2.cloned.1.call-done = bf16[2,4096,128]{2,1,0:T(8,128)(2,1)} async-done(((bf16[2,128,128]{2,1,0:T(8,128)(2,1)}), bf16[2,4096,128]{2,1,0:T(8,128)(2,1)}) %all-gather.2.cloned.1.call-update) | async-done | bytes 2097168 | tf_op jit(solution)/shard_map/all_gather | solution.py:101
  171.5 163.6 %while.14 = (s32[]{:T(128)}, f32[2048,128]{1,0:T(8,128)}, f32[4096]{0:T(1024)S(1)}, f32[2,1024]{1,0:T(2,128)S(1)}, f32[2,4096]{1,0:T(2,128)S(1)}, /*index=5*/bf1...) while((s32[]{:T(128)}, f32[2048,128]{1,0:T(8,128)}, ...), condition=%wide.region_2.0_spmd.clone, body=%wide.region_1.0_spmd.clone.sunk | while | flops 551551488 | bytes 51161332 | solution.py:62
  174.0 6.3 copy.58
  180.3 5.4 copy.59
  185.7 1.7 constant_dynamic-slice_fusion.5
  187.4 3.5 convolution_add_fusion.3
  194.4 6.3 copy.58
  200.7 5.4 copy.59
  206.2 1.7 constant_dynamic-slice_fusion.5
  207.8 3.5 convolution_add_fusion.3
  214.9 6.3 copy.58
  221.2 5.4 copy.59
  226.6 1.7 constant_dynamic-slice_fusion.5
  228.3 3.5 convolution_add_fusion.3
  235.3 6.3 copy.58
  241.6 5.4 copy.59
  247.1 1.7 constant_dynamic-slice_fusion.5
  248.7 3.5 convolution_add_fusion.3
  255.8 6.3 copy.58
  262.1 5.4 copy.59
  267.5 1.7 constant_dynamic-slice_fusion.5
  269.2 3.5 convolution_add_fusion.3
  276.2 6.3 copy.58
  282.5 5.4 copy.59
  288.0 1.7 constant_dynamic-slice_fusion.5
  289.6 3.5 convolution_add_fusion.3
  296.7 6.3 copy.58
  303.0 5.4 copy.59
  308.4 1.7 constant_dynamic-slice_fusion.5
  310.1 3.5 convolution_add_fusion.3
  317.1 6.3 copy.58
  323.4 5.4 copy.59
  330.5 3.5 convolution_add_fusion.3
  335.3 2.4 collective-permute-start
  337.7 8.7 %collective-permute-start.1 = (bf16[2,64,128]{2,1,0:T(8,128)(2,1)S(1)}, bf16[2,64,128]{2,1,0:T(8,128)(2,1)S(1)}, u32[]{:S(2)}, u32[]{:S(2)}) collective-permute-start(bf16[2,64,128]{2,1,0:T(8,128)(2,1)S(1)} %get-tuple-element.167), channel_id=1, source_target_pairs={{1,0},{2,1},{3,2},{4,3},{5,4},{6,5},{7,6},{8,7},{9,8},{10,9},{11,1... | collective-permute-start | bytes 98312 | tf_op jit(solution)/shard_map/ppermute | solution.py:22
  352.0 17.6 %reduce-scatter.5.cloned.1.call-done = f32[2,128,128]{2,1,0:T(8,128)} async-done(((f32[2,1024,128]{2,1,0:T(8,128)}), f32[2,128,128]{2,1,0:T(8,128)}) %reduce-scatter.5.cloned.1.call-update) | async-done | bytes 131088 | tf_op jit(solution)/shard_map/reduce_scatter | solution.py:102
  370.6 1.8 convolution_bitcast_fusion
  372.4 64.7 %all-reduce.4.cloned.1.call-done = f32[4,128,128]{2,1,0:T(8,128)} async-done(((f32[4,128,128]{2,1,0:T(8,128)}), f32[4,128,128]{2,1,0:T(8,128)}) %all-reduce.4.cloned.1.call-update) | async-done | bytes 262160 | tf_op jit(solution)/shard_map/psum | solution.py:127
  437.4 145.4 %all-reduce.6.cloned.1.call-done = f32[4,128,128]{2,1,0:T(8,128)} async-done(((f32[4,128,128]{2,1,0:T(8,128)}), f32[4,128,128]{2,1,0:T(8,128)}) %all-reduce.6.cloned.1.call-update) | async-done | bytes 262160 | tf_op jit(solution)/shard_map/psum | solution.py:126
  585.5 246.5 %all-reduce.8.cloned.1.call-done = f32[128,128]{0,1:T(8,128)} async-done(((f32[128,128]{0,1:T(8,128)}), f32[128,128]{0,1:T(8,128)}) %all-reduce.8.cloned.1.call-update) | async-done | bytes 65552 | tf_op jit(solution)/shard_map/psum | solution.py:134
  833.7 11.7 %cholesky.16 = f32[128,128]{1,0:T(8,128)S(1)} custom-call(f32[128,128]{1,0:T(8,128)S(1)} %fusion.27), custom_call_target="Cholesky" | custom-call | tf_op jit(solution)/shard_map/jit(cholesky)/cholesky | solution.py:135
  846.8 9.8 %custom-call.7 = f32[1,128,128]{1,2,0:T(8,128)S(1)} custom-call(f32[1,128,128]{2,1,0:T(8,128)S(1)} %get-tuple-element.165), custom_call_target="InvertDiagBlocksLowerTriangular" | custom-call | tf_op jit(solution)/shard_map/jit(_solve_triangular)/triangular_solve | solution.py:137
  (141 shorter events, 46.1 us)
Async XLA Ops:
  7.2 43.7 %copy-start = (f32[8,48,1536]{2,1,0:T(8,128)S(1)}, f32[8,48,1536]{2,1,0:T(8,128)}, u32[]{:S(2)}) copy-start(f32[8,48,1536]{2,1,0:T(8,128)} %param.19) | copy-start | bytes 7077892
  7.2 86.8 %reduce-scatter.3.cloned.1.call-start = ((), (), s32[]{:S(2)}) async-start(), calls=%async_computation.2 | async-start | bytes 221184 | tf_op jit(solution)/shard_map/reduce_scatter | solution.py:95
  8.5 85.5 %copy-start.7 = (s32[2,128]{1,0:T(2,128)S(1)}, s32[2,128]{1,0:T(2,128)}, u32[]{:S(2)}) copy-start(s32[2,128]{1,0:T(2,128)} %param.18) | copy-start | bytes 3076
  8.5 85.5 %copy-start.10 = (f32[2,128]{1,0:T(2,128)S(1)}, f32[2,128]{1,0:T(2,128)}, u32[]{:S(2)}) copy-start(f32[2,128]{1,0:T(2,128)} %param.14) | copy-start | bytes 3076
  50.9 45.1 %copy-start.6 = (f32[128]{0:T(128)S(1)}, f32[128]{0:T(128)}, u32[]{:S(2)}) copy-start(f32[128]{0:T(128)} %param.12) | copy-start | bytes 1540
  50.9 45.1 %copy-start.8 = (f32[2,128]{1,0:T(2,128)S(1)}, f32[2,128]{1,0:T(2,128)}, u32[]{:S(2)}) copy-start(f32[2,128]{1,0:T(2,128)} %param.11) | copy-start | bytes 3076
  53.6 117.9 %all-gather.2.cloned.1.call-start = ((), (), s32[]{:S(2)}) async-start(), calls=%async_computation.3 | async-start | bytes 2162688 | tf_op jit(solution)/shard_map/all_gather | solution.py:101
  95.9 273.8 %reduce-scatter.5.cloned.1.call-start = ((), (), s32[]{:S(2)}) async-start(), calls=%async_computation.4 | async-start | bytes 1179648 | tf_op jit(solution)/shard_map/reduce_scatter | solution.py:102
  171.5 163.7 %copy-start.9 = (s32[8,12]{1,0:T(8,128)S(1)}, s32[8,12]{1,0:T(8,128)}, u32[]{:S(2)}) copy-start(s32[8,12]{1,0:T(8,128)} %param.15) | copy-start | bytes 1156
  171.5 163.8 %copy-start.11 = (s32[8]{0:T(128)S(1)}, s32[8]{0:T(128)}, u32[]{:S(2)}) copy-start(s32[8]{0:T(128)} %param.16) | copy-start | bytes 100
  171.5 163.8 %copy-start.4 = (bf16[2,128,128]{2,1,0:T(8,128)(2,1)S(1)}, bf16[2,128,128]{2,1,0:T(8,128)(2,1)}, u32[]{:S(2)}) copy-start(bf16[2,128,128]{2,1,0:T(8,128)(2,1)} %fusion.16) | copy-start | bytes 196612
  180.3 7.1 copy-start.1
  190.9 1.0 copy-start.2
  200.7 7.1 copy-start.1
  211.4 1.0 copy-start.2
  221.2 7.1 copy-start.1
  231.8 1.0 copy-start.2
  241.6 7.1 copy-start.1
  252.3 1.0 copy-start.2
  262.1 7.1 copy-start.1
  272.7 1.0 copy-start.2
  282.5 7.1 copy-start.1
  293.2 1.0 copy-start.2
  303.0 7.1 copy-start.1
  313.6 1.0 copy-start.2
  323.4 7.1 copy-start.1
  334.1 1.0 copy-start.2
  335.1 102.0 %all-reduce.4.cloned.1.call-start = ((), (), s32[]{:S(2)}) async-start(), calls=%async_computation.5 | async-start | bytes 524288 | tf_op jit(solution)/shard_map/psum | solution.py:127
  335.3 11.1 %collective-permute-start = (bf16[2,64,128]{2,1,0:T(8,128)(2,1)S(1)}, bf16[2,64,128]{2,1,0:T(8,128)(2,1)S(1)}, u32[]{:S(2)}, u32[]{:S(2)}) collective-permute-start(bf16[2,64,128]{2,1,0:T(8,128)(2,1)S(1)} %get-tuple-element.166), channel_id=1, source_target_pairs={{0,1},{1,2},{2,3},{3,4},{4,5},{5,6},{6,7},{7,8},{8,9},{9,10},{10,1... | collective-permute-start | bytes 98312 | tf_op jit(solution)/shard_map/ppermute | solution.py:19
  337.7 9.7 %collective-permute-start.1 = (bf16[2,64,128]{2,1,0:T(8,128)(2,1)S(1)}, bf16[2,64,128]{2,1,0:T(8,128)(2,1)S(1)}, u32[]{:S(2)}, u32[]{:S(2)}) collective-permute-start(bf16[2,64,128]{2,1,0:T(8,128)(2,1)S(1)} %get-tuple-element.167), channel_id=1, source_target_pairs={{1,0},{2,1},{3,2},{4,3},{5,4},{6,5},{7,6},{8,7},{9,8},{10,9},{11,1... | collective-permute-start | bytes 98312 | tf_op jit(solution)/shard_map/ppermute | solution.py:22
  349.0 21.5 %copy-start.3 = (f32[4,2,128,128]{3,2,1,0:T(8,128)S(1)}, f32[4,2,128,128]{3,2,1,0:T(8,128)}, u32[]{:S(2)}) copy-start(f32[4,2,128,128]{3,2,1,0:T(8,128)} %param.13) | copy-start | bytes 1572868
  372.4 210.4 %all-reduce.6.cloned.1.call-start = ((), (), s32[]{:S(2)}) async-start(), calls=%async_computation.6 | async-start | bytes 524288 | tf_op jit(solution)/shard_map/psum | solution.py:126
  437.1 394.8 %all-reduce.8.cloned.1.call-start = ((), (), s32[]{:S(2)}) async-start(), calls=%async_computation.7 | async-start | bytes 131072 | tf_op jit(solution)/shard_map/psum | solution.py:134
  582.8 275.5 %copy-start.5 = (f32[4,128,128]{2,1,0:T(8,128)S(1)}, f32[4,128,128]{2,1,0:T(8,128)}, u32[]{:S(2)}) copy-start(f32[4,128,128]{2,1,0:T(8,128)} %all-reduce.6.cloned.1.call-done) | copy-start | bytes 786436
Sparse Core Ops, SparseCore 0:
  53.7 40.2 reduce-scatter.2
  97.1 74.2 all-gather.1
  335.2 34.3 reduce-scatter.4
  372.5 64.5 all-reduce.3
  440.4 142.3 all-reduce.5
  588.7 243.1 all-reduce.7
